TPU v7x, 512 devices: a whole 4x8x8 slice. The times are simulated.
512 devices in a mesh: panel: 2 (over y_lo), lon: 16 (over z, core), lat: 16 (over y_hi, x).
Axes of the slice: x: 4, y: 8 (y_hi: 4, y_lo: 2; y = y_hi * 2 + y_lo), z: 8, core: 2. Of those that a mesh axis runs over, the one named last changes fastest.
Arguments:
- pressure: float32 [2, 256, 512, 128], P('panel', 'lat', 'lon'), may hold values from -6 to 6
- porosity: float32 [2, 256, 512, 128], P('panel', 'lat', 'lon'), may hold values from 0.5 to 2
- source: float32 [2, 256, 512, 128], P('panel', 'lat', 'lon'), may hold values from -6 to 6
- bulk: float32 [2, 256, 512, 128], P('panel', 'lat', 'lon'), may hold values from 0.5 to 2
- lat_codes: int32 [2, 2, 2, 512], P('panel', None, None, 'lon'), may hold values from 0 to 8158, as said below
- lat_weights: float32 [2, 4, 2, 2, 512], P('panel', None, None, None, 'lon'), may hold values from 0 to 1, as said below
- lon_codes: int32 [2, 2, 2, 256], P('panel', None, None, 'lat'), may hold values from 0 to 8174, as said below
- lon_weights: float32 [2, 4, 2, 2, 256], P('panel', None, None, None, 'lat'), may hold values from 0 to 1, as said below
Outputs:
- pressure_out: float32 [2, 256, 512, 128], P('panel', 'lat', 'lon')
- porosity_out: float32 [2, 256, 512, 128], P('panel', 'lat', 'lon')
Inputs may be any that keep to these rules, and one draw needn't show every extreme that they name: `lat_codes`: an intersection map of the shell, which may differ from draw to draw: code = a * 32 + c with a < 255 a latitude of the whole panel and c < 31 an offset inside the longitude block of the ghost cell. `lon_codes`: an intersection map of the shell, which may differ from draw to draw: code = b * 16 + r with b < 511 a longitude of the whole panel and r < 15 an offset inside the latitude block of the ghost cell. `lat_weights`: the four weights of a ghost cell are non-negative and sum to one. `lon_weights`: the four weights of a ghost cell are non-negative and sum to one.
All inputs are finite; a program needn't handle non-finite values.
Results may differ from a plain program's by a relative error of at most 0.0003.
Values sent between devices are 32-bit elements; how exact they have to be, the bound alone decides.
A program may use at most 64 MiB of HBM per device.

v0:
```python
import jax
import jax.numpy as jnp
from jax import lax
from jax.sharding import PartitionSpec as P

SWEEPS = 3
stencil_offsets = ((0, 0), (0, 1), (1, 0), (1, 1))
radial_weight = 0.25
buoyancy = 0.5
time_step = 0.04


def padded_2(cells, sides, width):
    for axis, dim in sides:
        count = lax.axis_size(axis)
        ends = count - 1
        head = lax.slice_in_dim(cells, 0, width, axis=dim)
        tail = lax.slice_in_dim(cells, cells.shape[dim] - width, cells.shape[dim], axis=dim)
        cells = jnp.concatenate(
            [
                lax.ppermute(tail, axis, [(i, (i + 1) % count) for i in range(ends)]),
                cells,
                lax.ppermute(head, axis, [((i + 1) % count, i) for i in range(ends)]),
            ],
            axis=dim,
        )
    return cells


def swapped(block, axis, distance):
    count = lax.axis_size(axis)
    route = []
    for low in range(count):
        high = low | 1 << distance
        if high != low and high < count:
            route += [(low, high), (high, low)]
    return lax.ppermute(block, axis, route)


def pad_last(values, before, after):
    widths = [(0, 0)] * (values.ndim - 1) + [(before, after)]
    return jnp.pad(values, widths)


def rim_terms(field, lat_codes, lat_weights, lon_codes, lon_weights, width):
    rows_dev, cols_dev, levels = field.shape
    first_row = lax.axis_index("lat") * rows_dev
    first_col = lax.axis_index("lon") * cols_dev
    chosen = lat_codes[:, :width]
    rows_at = chosen // cols_dev - first_row
    cols_at = chosen % cols_dev
    lat_total = jnp.zeros(chosen.shape + (levels,), jnp.float32)
    for corner, (row_step, col_step) in enumerate(stencil_offsets):
        target = rows_at + row_step
        inside = (target >= 0) & (target < rows_dev)
        picked = field[jnp.clip(target, 0, rows_dev - 1), cols_at + col_step]
        lat_total = (
            lat_total + jnp.where(inside, lat_weights[corner, :, :width], 0.0)[..., None] * picked
        )
    chosen = lon_codes[:, :width]
    cols_at = chosen // rows_dev - first_col
    rows_at = chosen % rows_dev
    lon_total = jnp.zeros(chosen.shape + (levels,), jnp.float32)
    for corner, (row_step, col_step) in enumerate(stencil_offsets):
        target = cols_at + col_step
        inside = (target >= 0) & (target < cols_dev)
        picked = field[rows_at + row_step, jnp.clip(target, 0, cols_dev - 1)]
        lon_total = (
            lon_total + jnp.where(inside, lon_weights[corner, :, :width], 0.0)[..., None] * picked
        )
    return (lat_total, lon_total)


def surround(field, width, lat_codes, lat_weights, lon_codes, lon_weights):
    rows_dev, cols_dev, levels = field.shape
    padded = padded_2(field, (("lat", 0), ("lon", 1)), width)
    lat_terms, lon_terms = rim_terms(field, lat_codes, lat_weights, lon_codes, lon_weights, width)
    lat_summed = lax.psum(lat_terms, "lat")
    lon_summed = lax.psum(lon_terms, "lon")
    arrived = swapped(jnp.concatenate([lat_summed, lon_summed], axis=2), "panel", 0)
    lat_rim = arrived[:, :, :cols_dev]
    lon_rim = arrived[:, :, cols_dev:]
    lat_index = lax.axis_index("lat")
    lon_index = lax.axis_index("lon")
    last_lat = lax.axis_size("lat") - 1
    last_lon = lax.axis_size("lon") - 1
    north = jnp.where(lat_index == 0, lat_rim[0][::-1], padded[:width, width : width + cols_dev])
    padded = padded.at[:width, width : width + cols_dev].set(north)
    south = jnp.where(
        lat_index == last_lat, lat_rim[1], padded[width + rows_dev :, width : width + cols_dev]
    )
    padded = padded.at[width + rows_dev :, width : width + cols_dev].set(south)
    west = jnp.where(
        lon_index == 0,
        jnp.moveaxis(lon_rim[0][::-1], 0, 1),
        padded[width : width + rows_dev, :width],
    )
    padded = padded.at[width : width + rows_dev, :width].set(west)
    east = jnp.where(
        lon_index == last_lon,
        jnp.moveaxis(lon_rim[1], 0, 1),
        padded[width : width + rows_dev, width + cols_dev :],
    )
    padded = padded.at[width : width + rows_dev, width + cols_dev :].set(east)
    return padded


def face_terms(mobility):
    lat_face = 0.5 * (mobility[..., :-1, 1:-1, :] + mobility[..., 1:, 1:-1, :])
    lon_face = 0.5 * (mobility[..., 1:-1, :-1, :] + mobility[..., 1:-1, 1:, :])
    inner = mobility[..., 1:-1, 1:-1, :]
    mean_rad = 0.5 * (inner[..., :-1] + inner[..., 1:])
    return (lat_face, lon_face, mean_rad)


def diagonal_sum(bulk, lat_face, lon_face, mean_rad):
    rad_face = radial_weight * mean_rad
    total = bulk + lat_face[..., :-1, :, :] + lat_face[..., 1:, :, :]
    total = total + lon_face[..., :, :-1, :] + lon_face[..., :, 1:, :]
    return total + pad_last(rad_face, 1, 0) + pad_last(rad_face, 0, 1)


def neighbour_total(padded, source, lat_face, lon_face, mean_rad):
    inner = padded[..., 1:-1, 1:-1, :]
    rad_face = radial_weight * mean_rad
    total = source + lat_face[..., :-1, :, :] * padded[..., :-2, 1:-1, :]
    total = total + lat_face[..., 1:, :, :] * padded[..., 2:, 1:-1, :]
    total = total + lon_face[..., :, :-1, :] * padded[..., 1:-1, :-2, :]
    total = total + lon_face[..., :, 1:, :] * padded[..., 1:-1, 2:, :]
    total = (
        total
        + pad_last(rad_face * inner[..., :-1], 1, 0)
        + pad_last(rad_face * inner[..., 1:], 0, 1)
    )
    return total


def advect(pressure_pad, porosity_pad, lat_face, lon_face, mean_rad, bulk):
    pressure_in = pressure_pad[..., 1:-1, 1:-1, :]
    porosity_in = porosity_pad[..., 2:-2, 2:-2, :]
    lat_speed = -lat_face * (pressure_pad[..., 1:, 1:-1, :] - pressure_pad[..., :-1, 1:-1, :])
    lat_left = 1.5 * porosity_pad[..., 1:-2, 2:-2, :] - 0.5 * porosity_pad[..., :-3, 2:-2, :]
    lat_right = 1.5 * porosity_pad[..., 2:-1, 2:-2, :] - 0.5 * porosity_pad[..., 3:, 2:-2, :]
    lat_flux = lat_speed * jnp.where(lat_speed > 0, lat_left, lat_right)
    lon_speed = -lon_face * (pressure_pad[..., 1:-1, 1:, :] - pressure_pad[..., 1:-1, :-1, :])
    lon_left = 1.5 * porosity_pad[..., 2:-2, 1:-2, :] - 0.5 * porosity_pad[..., 2:-2, :-3, :]
    lon_right = 1.5 * porosity_pad[..., 2:-2, 2:-1, :] - 0.5 * porosity_pad[..., 2:-2, 3:, :]
    lon_flux = lon_speed * jnp.where(lon_speed > 0, lon_left, lon_right)
    rad_speed = (
        -radial_weight * mean_rad * (pressure_in[..., 1:] - pressure_in[..., :-1])
        + buoyancy * mean_rad
    )
    rad_flux = rad_speed * jnp.where(rad_speed > 0, porosity_in[..., :-1], porosity_in[..., 1:])
    divergence = lat_flux[..., 1:, :, :] - lat_flux[..., :-1, :, :]
    divergence = divergence + lon_flux[..., :, 1:, :] - lon_flux[..., :, :-1, :]
    divergence = divergence + pad_last(rad_flux, 0, 1) - pad_last(rad_flux, 1, 0)
    return porosity_in - time_step * (divergence + bulk * pressure_in)


def body(pressure, porosity, source, bulk, lat_codes, lat_weights, lon_codes, lon_weights):
    current = pressure[0]
    porosity_now = porosity[0]
    source_now = source[0]
    bulk_now = bulk[0]
    lat_code_now = lat_codes[0]
    lat_weight_now = lat_weights[0]
    lon_code_now = lon_codes[0]
    lon_weight_now = lon_weights[0]
    porosity_pad = surround(
        porosity_now, 2, lat_code_now, lat_weight_now, lon_code_now, lon_weight_now
    )
    near = porosity_pad[1:-1, 1:-1, :]
    mobility = near * near * near
    lat_face, lon_face, mean_rad = face_terms(mobility)
    denominator = diagonal_sum(bulk_now, lat_face, lon_face, mean_rad)
    for sweep_index in range(SWEEPS):
        padded = surround(current, 1, lat_code_now, lat_weight_now, lon_code_now, lon_weight_now)
        current = neighbour_total(padded, source_now, lat_face, lon_face, mean_rad) / denominator
    pressure_pad = surround(current, 1, lat_code_now, lat_weight_now, lon_code_now, lon_weight_now)
    porosity_new = advect(pressure_pad, porosity_pad, lat_face, lon_face, mean_rad, bulk_now)
    return (current[None], porosity_new[None])


def solution(mesh):
    placed = (
        P("panel", "lat", "lon", None),
        P("panel", "lat", "lon", None),
        P("panel", "lat", "lon", None),
        P("panel", "lat", "lon", None),
        P("panel", None, None, "lon"),
        P("panel", None, None, None, "lon"),
        P("panel", None, None, "lat"),
        P("panel", None, None, None, "lat"),
    )
    return jax.shard_map(
        body,
        mesh=mesh,
        in_specs=placed,
        out_specs=(P("panel", "lat", "lon", None), P("panel", "lat", "lon", None)),
        check_vma=False,
    )
```

profile of v0, /device:TPU:296, one launch (start us, length us, event | category | flops | bytes accessed | tf_op | source)
XLA Modules:
  0.0 695.2 jit_solution(16272074655665553990)
XLA Ops:
  8.1 1.9 gather_fusion.1
  10.0 1.2 gather_fusion.2
  11.3 1.2 gather_fusion.3
  12.6 1.2 gather_fusion
  14.9 3.5 collective-permute-start
  18.5 6.7 collective-permute-start.1
  36.6 76.8 %psum.72 = f32[2,1,32,128]{3,2,1,0:T(8,128)S(1)} all-reduce(f32[2,1,32,128]{3,2,1,0:T(8,128)S(1)} %multiply_add_fusion.4), channel_id=1, replica_groups=mesh['panel'=2,'lon'=16,'lat'=16] {'lat'}, use_global_device_ids=true, to_apply=%region_3.4 | all-reduce | flops 8192 | bytes 65536 | tf_op jit(solution)/shard_map/psum | solution.py:78
  113.6 47.4 %all-reduce.10 = (f32[2,1,16,128]{3,2,1,0:T(8,128)S(1)}, f32[2,2,16,128]{3,2,1,0:T(8,128)S(1)}) all-reduce(f32[2,1,16,128]{3,2,1,0:T(8,128)S(1)} %multiply_add_fusion.9, f32[2,2,16,128]{3,2,1,0:T(8,128)S(1)} %multiply_add_fusion.5), channel_id=1, replica_groups=mesh['panel'=2,'lon'=16,'lat'=16] {'lon'}, use_global_device_ids=true, to_apply=%region_4.5 | all-reduce | flops 12288 | bytes 98304 | tf_op jit(solution)/shard_map/psum | solution.py:79
  160.9 3.3 collective-permute-start.9
  164.2 1.9 collective-permute-start.5
  166.2 8.1 %collective-permute-start.6 = (f32[1,32,128]{2,1,0:T(8,128)S(1)}, f32[1,32,128]{2,1,0:T(8,128)S(1)}, u32[]{:S(2)}, u32[]{:S(2)}) collective-permute-start(f32[1,32,128]{2,1,0:T(8,128)S(1)} %get-tuple-element.306), channel_id=1, source_target_pairs={{1,0},{2,1},{3,2},{4,3},{5,4},{6,5},{7,6},{8,7},{9,8},{10,9},{11,1... | collective-permute-start | bytes 49160 | tf_op jit(solution)/shard_map/ppermute | solution.py:23
  175.8 1.9 collective-permute-start.7
  177.7 4.9 collective-permute-start.8
  184.0 1.9 collective-permute-start.2
  185.9 4.9 collective-permute-start.3
  190.8 1.4 scatter.74
  193.5 2.7 collective-permute-start.4
  196.3 3.7 collective-permute-done.4
  200.1 2.0 dynamic-slice_select_fusion
  202.1 1.5 scatter.66
  213.8 1.2 fusion.127
  216.2 83.2 %psum.74 = f32[2,1,32,128]{3,2,1,0:T(8,128)S(1)} all-reduce(f32[2,1,32,128]{3,2,1,0:T(8,128)S(1)} %multiply_add_fusion.3), channel_id=1, replica_groups=mesh['panel'=2,'lon'=16,'lat'=16] {'lat'}, use_global_device_ids=true, to_apply=%region_5.6 | all-reduce | flops 8192 | bytes 65536 | tf_op jit(solution)/shard_map/psum | solution.py:78
  299.4 1.9 collective-permute-start.10
  301.3 8.1 %collective-permute-start.11 = (f32[1,32,128]{2,0,1:T(1,128)S(1)}, f32[1,32,128]{2,0,1:T(1,128)S(1)}, u32[]{:S(2)}, u32[]{:S(2)}) collective-permute-start(f32[1,32,128]{2,0,1:T(1,128)S(1)} %slice.1292), channel_id=1, source_target_pairs={{1,0},{2,1},{3,2},{4,3},{5,4},{6,5},{7,6},{8,7},{9,8},{10,9},{11,1... | collective-permute-start | bytes 49160 | tf_op jit(solution)/shard_map/ppermute | solution.py:23
  309.5 45.7 %psum.75 = f32[2,1,16,128]{3,2,1,0:T(8,128)S(1)} all-reduce(f32[2,1,16,128]{3,2,1,0:T(8,128)S(1)} %multiply_add_fusion.8), channel_id=1, replica_groups=mesh['panel'=2,'lon'=16,'lat'=16] {'lon'}, use_global_device_ids=true, to_apply=%region_6.7 | all-reduce | flops 4096 | bytes 32768 | tf_op jit(solution)/shard_map/psum | solution.py:79
  355.3 1.9 collective-permute-start.12
  357.2 4.9 collective-permute-start.13
  362.1 2.6 collective-permute-start.14
  364.8 3.3 collective-permute-done.14
  368.1 1.3 scatter.80
  378.7 76.9 %psum.76 = f32[2,1,32,128]{3,2,1,0:T(8,128)S(1)} all-reduce(f32[2,1,32,128]{3,2,1,0:T(8,128)S(1)} %multiply_add_fusion.2), channel_id=1, replica_groups=mesh['panel'=2,'lon'=16,'lat'=16] {'lat'}, use_global_device_ids=true, to_apply=%region_7.8 | all-reduce | flops 8192 | bytes 65536 | tf_op jit(solution)/shard_map/psum | solution.py:78
  455.6 1.9 collective-permute-start.15
  457.5 8.1 %collective-permute-start.16 = (f32[1,32,128]{2,0,1:T(1,128)S(1)}, f32[1,32,128]{2,0,1:T(1,128)S(1)}, u32[]{:S(2)}, u32[]{:S(2)}) collective-permute-start(f32[1,32,128]{2,0,1:T(1,128)S(1)} %slice.1307), channel_id=1, source_target_pairs={{1,0},{2,1},{3,2},{4,3},{5,4},{6,5},{7,6},{8,7},{9,8},{10,9},{11,1... | collective-permute-start | bytes 49160 | tf_op jit(solution)/shard_map/ppermute | solution.py:23
  465.7 45.7 %psum.77 = f32[2,1,16,128]{3,2,1,0:T(8,128)S(1)} all-reduce(f32[2,1,16,128]{3,2,1,0:T(8,128)S(1)} %multiply_add_fusion.7), channel_id=1, replica_groups=mesh['panel'=2,'lon'=16,'lat'=16] {'lon'}, use_global_device_ids=true, to_apply=%region_8.9 | all-reduce | flops 4096 | bytes 32768 | tf_op jit(solution)/shard_map/psum | solution.py:79
  511.5 1.9 collective-permute-start.17
  513.4 4.9 collective-permute-start.18
  518.3 2.4 collective-permute-start.19
  520.8 3.5 collective-permute-done.19
  524.3 1.3 scatter.86
  535.2 76.8 %psum.78 = f32[2,1,32,128]{3,2,1,0:T(8,128)S(1)} all-reduce(f32[2,1,32,128]{3,2,1,0:T(8,128)S(1)} %multiply_add_fusion.1), channel_id=1, replica_groups=mesh['panel'=2,'lon'=16,'lat'=16] {'lat'}, use_global_device_ids=true, to_apply=%region_9.10 | all-reduce | flops 8192 | bytes 65536 | tf_op jit(solution)/shard_map/psum | solution.py:78
  611.9 1.9 collective-permute-start.20
  613.9 8.1 %collective-permute-start.21 = (f32[1,32,128]{2,0,1:T(1,128)S(1)}, f32[1,32,128]{2,0,1:T(1,128)S(1)}, u32[]{:S(2)}, u32[]{:S(2)}) collective-permute-start(f32[1,32,128]{2,0,1:T(1,128)S(1)} %slice.1323), channel_id=1, source_target_pairs={{1,0},{2,1},{3,2},{4,3},{5,4},{6,5},{7,6},{8,7},{9,8},{10,9},{11,1... | collective-permute-start | bytes 49160 | tf_op jit(solution)/shard_map/ppermute | solution.py:23
  622.1 45.7 %psum.79 = f32[2,1,16,128]{3,2,1,0:T(8,128)S(1)} all-reduce(f32[2,1,16,128]{3,2,1,0:T(8,128)S(1)} %multiply_add_fusion.6), channel_id=1, replica_groups=mesh['panel'=2,'lon'=16,'lat'=16] {'lon'}, use_global_device_ids=true, to_apply=%region_10.11 | all-reduce | flops 4096 | bytes 32768 | tf_op jit(solution)/shard_map/psum | solution.py:79
  667.9 1.9 collective-permute-start.22
  669.8 4.9 collective-permute-start.23
  674.7 2.4 collective-permute-start.24
  678.0 2.7 collective-permute-done.24
  680.7 1.3 scatter.94
  (268 shorter events, 55.2 us)
Async XLA Ops:
  7.2 185.5 %all-reduce.13.cloned.1.call-start = ((), (), s32[]{:S(2)}) async-start(), calls=%async_computation | async-start | bytes 131072 | tf_op jit(solution)/shard_map/psum | solution.py:78
  8.1 1.9 copy-start
  12.6 1.2 copy-start.19
  14.7 10.4 %copy-start.20 = (f32[1,4,2,2,16]{4,3,2,1,0:T(2,128)S(1)}, f32[1,4,2,2,16]{4,3,2,1,0:T(2,128)}, u32[]{:S(2)}) copy-start(f32[1,4,2,2,16]{4,3,2,1,0:T(2,128)} %param.55) | copy-start | bytes 3076
  14.7 10.4 %copy-start.21 = (s32[1,2,2,16]{3,2,1,0:T(2,128)S(1)}, s32[1,2,2,16]{3,2,1,0:T(2,128)}, u32[]{:S(2)}) copy-start(s32[1,2,2,16]{3,2,1,0:T(2,128)} %param.54) | copy-start | bytes 772
  14.9 10.7 %copy-start.1 = (f32[1,16,32,128]{3,2,1,0:T(8,128)S(1)}, f32[1,16,32,128]{3,2,1,0:T(8,128)}, u32[]{:S(2)}) copy-start(f32[1,16,32,128]{3,2,1,0:T(8,128)} %param.48) | copy-start | bytes 786436
  14.9 169.0 %collective-permute-start = (f32[2,32,128]{2,0,1:T(2,128)S(1)}, f32[2,32,128]{2,0,1:T(2,128)S(1)}, u32[]{:S(2)}, u32[]{:S(2)}) collective-permute-start(f32[2,32,128]{2,0,1:T(2,128)S(1)} %get-tuple-element.301), channel_id=1, source_target_pairs={{0,1},{1,2},{2,3},{3,4},{4,5},{5,6},{6,7},{7,8},{8,9},{9,10},{10,1... | collective-permute-start | bytes 98312 | tf_op jit(solution)/shard_map/ppermute | solution.py:21
  18.5 165.5 %collective-permute-start.1 = (f32[2,32,128]{2,0,1:T(2,128)S(1)}, f32[2,32,128]{2,0,1:T(2,128)S(1)}, u32[]{:S(2)}, u32[]{:S(2)}) collective-permute-start(f32[2,32,128]{2,0,1:T(2,128)S(1)} %get-tuple-element.302), channel_id=1, source_target_pairs={{1,0},{2,1},{3,2},{4,3},{5,4},{6,5},{7,6},{8,7},{9,8},{10,9},{11,1... | collective-permute-start | bytes 98312 | tf_op jit(solution)/shard_map/ppermute | solution.py:23
  160.9 29.8 %collective-permute-start.9 = (f32[2,1,48,128]{3,2,1,0:T(8,128)S(1)}, f32[2,1,48,128]{3,2,1,0:T(8,128)S(1)}, u32[]{:S(2)}, u32[]{:S(2)}) collective-permute-start(f32[2,1,48,128]{3,2,1,0:T(8,128)S(1)} %pad_maximum_fusion.6), channel_id=1, source_target_pairs={{0,256},{256,0},{1,257},{257,1},{2,258},{258,2},{3,259},{259,3},{4... | collective-permute-start | bytes 147464 | tf_op jit(solution)/shard_map/ppermute | solution.py:37
  164.2 11.5 %collective-permute-start.5 = (f32[1,32,128]{2,1,0:T(8,128)S(1)}, f32[1,32,128]{2,1,0:T(8,128)S(1)}, u32[]{:S(2)}, u32[]{:S(2)}) collective-permute-start(f32[1,32,128]{2,1,0:T(8,128)S(1)} %get-tuple-element.305), channel_id=1, source_target_pairs={{0,1},{1,2},{2,3},{3,4},{4,5},{5,6},{6,7},{7,8},{8,9},{9,10},{10,1... | collective-permute-start | bytes 49160 | tf_op jit(solution)/shard_map/ppermute | solution.py:21
  166.2 8.2 %copy-start.23 = (s32[3]{0:T(128)S(1)}, s32[3]{0:T(128)}, u32[]{:S(2)}) copy-start(s32[3]{0:T(128)} %constant.643.clone.1) | copy-start | bytes 40
  166.2 9.6 %collective-permute-start.6 = (f32[1,32,128]{2,1,0:T(8,128)S(1)}, f32[1,32,128]{2,1,0:T(8,128)S(1)}, u32[]{:S(2)}, u32[]{:S(2)}) collective-permute-start(f32[1,32,128]{2,1,0:T(8,128)S(1)} %get-tuple-element.306), channel_id=1, source_target_pairs={{1,0},{2,1},{3,2},{4,3},{5,4},{6,5},{7,6},{8,7},{9,8},{10,9},{11,1... | collective-permute-start | bytes 49160 | tf_op jit(solution)/shard_map/ppermute | solution.py:23
  175.8 7.4 %collective-permute-start.7 = (f32[18,1,128]{2,1,0:T(1,128)S(1)}, f32[18,1,128]{2,1,0:T(1,128)S(1)}, u32[]{:S(2)}, u32[]{:S(2)}) collective-permute-start(f32[18,1,128]{2,1,0:T(1,128)S(1)} %get-tuple-element.297), channel_id=1, source_target_pairs={{0,16},{16,32},{32,48},{48,64},{64,80},{80,96},{96,112},{112,128},... | collective-permute-start | bytes 27656 | tf_op jit(solution)/shard_map/ppermute | solution.py:21
  177.7 6.2 collective-permute-start.8
  184.0 12.2 %collective-permute-start.2 = (f32[20,2,128]{2,0,1:T(8,128)S(1)}, f32[20,2,128]{2,0,1:T(8,128)S(1)}, u32[]{:S(2)}, u32[]{:S(2)}) collective-permute-start(f32[20,2,128]{2,0,1:T(8,128)S(1)} %get-tuple-element.289), channel_id=1, source_target_pairs={{0,16},{16,32},{32,48},{48,64},{64,80},{80,96},{96,112},{112,128},... | collective-permute-start | bytes 61448 | tf_op jit(solution)/shard_map/ppermute | solution.py:21
  185.9 10.3 %collective-permute-start.3 = (f32[20,2,128]{2,0,1:T(8,128)S(1)}, f32[20,2,128]{2,0,1:T(8,128)S(1)}, u32[]{:S(2)}, u32[]{:S(2)}) collective-permute-start(f32[20,2,128]{2,0,1:T(8,128)S(1)} %get-tuple-element.290), channel_id=1, source_target_pairs={{16,0},{32,16},{48,32},{64,48},{80,64},{96,80},{112,96},{128,112},... | collective-permute-start | bytes 61448 | tf_op jit(solution)/shard_map/ppermute | solution.py:23
  193.5 6.5 collective-permute-start.4
  204.3 0.8 copy-start.4
  205.4 1.0 copy-start.6
  205.4 1.0 copy-start.17
  299.4 55.9 %collective-permute-start.10 = (f32[1,32,128]{2,1,0:T(8,128)S(1)}, f32[1,32,128]{2,1,0:T(8,128)S(1)}, u32[]{:S(2)}, u32[]{:S(2)}) collective-permute-start(f32[1,32,128]{2,1,0:T(8,128)S(1)} %slice.1291), channel_id=1, source_target_pairs={{0,1},{1,2},{2,3},{3,4},{4,5},{5,6},{6,7},{7,8},{8,9},{9,10},{10,1... | collective-permute-start | bytes 49160 | tf_op jit(solution)/shard_map/ppermute | solution.py:21
  301.3 54.0 %collective-permute-start.11 = (f32[1,32,128]{2,0,1:T(1,128)S(1)}, f32[1,32,128]{2,0,1:T(1,128)S(1)}, u32[]{:S(2)}, u32[]{:S(2)}) collective-permute-start(f32[1,32,128]{2,0,1:T(1,128)S(1)} %slice.1292), channel_id=1, source_target_pairs={{1,0},{2,1},{3,2},{4,3},{5,4},{6,5},{7,6},{8,7},{9,8},{10,9},{11,1... | collective-permute-start | bytes 49160 | tf_op jit(solution)/shard_map/ppermute | solution.py:23
  355.3 9.4 %collective-permute-start.12 = (f32[18,1,128]{2,0,1:T(8,128)S(1)}, f32[18,1,128]{2,0,1:T(8,128)S(1)}, u32[]{:S(2)}, u32[]{:S(2)}) collective-permute-start(f32[18,1,128]{2,0,1:T(8,128)S(1)} %get-tuple-element.295), channel_id=1, source_target_pairs={{0,16},{16,32},{32,48},{48,64},{64,80},{80,96},{96,112},{112,128},... | collective-permute-start | bytes 27656 | tf_op jit(solution)/shard_map/ppermute | solution.py:21
  357.2 7.5 %collective-permute-start.13 = (f32[18,1,128]{2,0,1:T(8,128)S(1)}, f32[18,1,128]{2,0,1:T(8,128)S(1)}, u32[]{:S(2)}, u32[]{:S(2)}) collective-permute-start(f32[18,1,128]{2,0,1:T(8,128)S(1)} %get-tuple-element.296), channel_id=1, source_target_pairs={{16,0},{32,16},{48,32},{64,48},{80,64},{96,80},{112,96},{128,112},... | collective-permute-start | bytes 27656 | tf_op jit(solution)/shard_map/ppermute | solution.py:23
  362.1 6.0 collective-permute-start.14
  370.0 1.0 copy-start.7
  455.6 55.9 %collective-permute-start.15 = (f32[1,32,128]{2,1,0:T(8,128)S(1)}, f32[1,32,128]{2,1,0:T(8,128)S(1)}, u32[]{:S(2)}, u32[]{:S(2)}) collective-permute-start(f32[1,32,128]{2,1,0:T(8,128)S(1)} %slice.1306), channel_id=1, source_target_pairs={{0,1},{1,2},{2,3},{3,4},{4,5},{5,6},{6,7},{7,8},{8,9},{9,10},{10,1... | collective-permute-start | bytes 49160 | tf_op jit(solution)/shard_map/ppermute | solution.py:21
  457.5 54.0 %collective-permute-start.16 = (f32[1,32,128]{2,0,1:T(1,128)S(1)}, f32[1,32,128]{2,0,1:T(1,128)S(1)}, u32[]{:S(2)}, u32[]{:S(2)}) collective-permute-start(f32[1,32,128]{2,0,1:T(1,128)S(1)} %slice.1307), channel_id=1, source_target_pairs={{1,0},{2,1},{3,2},{4,3},{5,4},{6,5},{7,6},{8,7},{9,8},{10,9},{11,1... | collective-permute-start | bytes 49160 | tf_op jit(solution)/shard_map/ppermute | solution.py:23
  511.5 9.2 %collective-permute-start.17 = (f32[18,1,128]{2,0,1:T(8,128)S(1)}, f32[18,1,128]{2,0,1:T(8,128)S(1)}, u32[]{:S(2)}, u32[]{:S(2)}) collective-permute-start(f32[18,1,128]{2,0,1:T(8,128)S(1)} %get-tuple-element.293), channel_id=1, source_target_pairs={{0,16},{16,32},{32,48},{48,64},{64,80},{80,96},{96,112},{112,128},... | collective-permute-start | bytes 27656 | tf_op jit(solution)/shard_map/ppermute | solution.py:21
  513.4 7.3 %collective-permute-start.18 = (f32[18,1,128]{2,0,1:T(8,128)S(1)}, f32[18,1,128]{2,0,1:T(8,128)S(1)}, u32[]{:S(2)}, u32[]{:S(2)}) collective-permute-start(f32[18,1,128]{2,0,1:T(8,128)S(1)} %get-tuple-element.294), channel_id=1, source_target_pairs={{16,0},{32,16},{48,32},{64,48},{80,64},{96,80},{112,96},{128,112},... | collective-permute-start | bytes 27656 | tf_op jit(solution)/shard_map/ppermute | solution.py:23
  518.3 6.0 collective-permute-start.19
  526.5 1.0 copy-start.8
  611.9 55.9 %collective-permute-start.20 = (f32[1,32,128]{2,1,0:T(8,128)S(1)}, f32[1,32,128]{2,1,0:T(8,128)S(1)}, u32[]{:S(2)}, u32[]{:S(2)}) collective-permute-start(f32[1,32,128]{2,1,0:T(8,128)S(1)} %slice.1322), channel_id=1, source_target_pairs={{0,1},{1,2},{2,3},{3,4},{4,5},{5,6},{6,7},{7,8},{8,9},{9,10},{10,1... | collective-permute-start | bytes 49160 | tf_op jit(solution)/shard_map/ppermute | solution.py:21
  613.9 54.0 %collective-permute-start.21 = (f32[1,32,128]{2,0,1:T(1,128)S(1)}, f32[1,32,128]{2,0,1:T(1,128)S(1)}, u32[]{:S(2)}, u32[]{:S(2)}) collective-permute-start(f32[1,32,128]{2,0,1:T(1,128)S(1)} %slice.1323), channel_id=1, source_target_pairs={{1,0},{2,1},{3,2},{4,3},{5,4},{6,5},{7,6},{8,7},{9,8},{10,9},{11,1... | collective-permute-start | bytes 49160 | tf_op jit(solution)/shard_map/ppermute | solution.py:23
  667.9 10.0 %collective-permute-start.22 = (f32[18,1,128]{2,0,1:T(8,128)S(1)}, f32[18,1,128]{2,0,1:T(8,128)S(1)}, u32[]{:S(2)}, u32[]{:S(2)}) collective-permute-start(f32[18,1,128]{2,0,1:T(8,128)S(1)} %get-tuple-element.291), channel_id=1, source_target_pairs={{0,16},{16,32},{32,48},{48,64},{64,80},{80,96},{96,112},{112,128},... | collective-permute-start | bytes 27656 | tf_op jit(solution)/shard_map/ppermute | solution.py:21
  669.8 8.1 %collective-permute-start.23 = (f32[18,1,128]{2,0,1:T(8,128)S(1)}, f32[18,1,128]{2,0,1:T(8,128)S(1)}, u32[]{:S(2)}, u32[]{:S(2)}) collective-permute-start(f32[18,1,128]{2,0,1:T(8,128)S(1)} %get-tuple-element.292), channel_id=1, source_target_pairs={{16,0},{32,16},{48,32},{64,48},{80,64},{96,80},{112,96},{128,112},... | collective-permute-start | bytes 27656 | tf_op jit(solution)/shard_map/ppermute | solution.py:23
  674.7 6.0 collective-permute-start.24
  677.9 4.6 copy-start.5
  678.0 4.5 copy-start.3
  683.0 1.0 copy-start.10
  683.0 1.1 copy-start.11
  683.0 1.2 copy-start.12
  683.1 1.3 copy-start.9
  684.4 1.0 copy-start.13
  684.4 1.0 copy-start.14
  684.4 1.1 copy-start.15
  684.4 1.2 copy-start.16
  686.2 1.0 copy-start.18
  (2 other events, 1.4 us)
Sparse Core Ops, SparseCore 0:
  14.8 158.6 all-reduce.12
where the time goes:
time: 696 us; the launch traced here: 695 us
  blocking collectives  498 us (72%)
  starting transfers between devices  97.7 us (14%)
  local copies, waits for them, and re-layouts  57.8 us (8%)
  between operations  15.5 us (2%)
  waiting for transfers between devices  13.9 us (2%)
  other arithmetic  12 us (2%)
    psum x4, blocking collectives, surround(): lat_summed = lax.psum(lat_terms, 'lat')  314 us
    psum x4, blocking collectives, surround(): lon_summed = lax.psum(lon_terms, 'lon')  185 us
    ppermute x10, starting transfers between devices, padded_2(): lax.ppermute(head, axis, [((i + 1) % count, i) for i in range(ends)])  63.5 us
    ppermute x10, starting transfers between devices, padded_2(): lax.ppermute(tail, axis, [(i, (i + 1) % count) for i in range(ends)])  20.8 us
    gather x20, local copies, waits for them, and re-layouts, rim_terms(): picked = field[jnp.clip(target, 0, rows_dev - 1), cols_at + col_step]  19.7 us
    gather x20, local copies, waits for them, and re-layouts, rim_terms(): picked = field[rows_at + row_step, jnp.clip(target, 0, cols_dev - 1)]  14.8 us
  transfers between devices with their start and end apart: 26, of which 5 were waited for; matrix products, arithmetic and copies ran while one was open for 3% of the time, Pallas kernels for 0%

commit v1 on v0

--- a/solution.py
+++ b/solution.py
@@ -75,7 +75,7 @@
     rows_dev, cols_dev, levels = field.shape
     padded = padded_2(field, (("lat", 0), ("lon", 1)), width)
     lat_terms, lon_terms = rim_terms(field, lat_codes, lat_weights, lon_codes, lon_weights, width)
-    lat_summed = lax.psum(lat_terms, "lat")
+    lat_summed = jnp.sum(lax.all_gather(lat_terms, "lat"), axis=0)
     lon_summed = lax.psum(lon_terms, "lon")
     arrived = swapped(jnp.concatenate([lat_summed, lon_summed], axis=2), "panel", 0)
     lat_rim = arrived[:, :, :cols_dev]

time: 696 us -> 583 us (0.84)
  the two profiles are of different devices: /device:TPU:296 before, /device:TPU:288 now
where the time goes in v1:
time: 583 us; the launch traced here: 582 us
  blocking collectives  356 us (61%)
  starting transfers between devices  96.2 us (17%)
  local copies, waits for them, and re-layouts  56.2 us (10%)
  waiting for transfers between devices  41.9 us (7%)
  other arithmetic  15.8 us (3%)
  between operations  15.5 us (3%)
    psum x4, blocking collectives, surround(): lon_summed = lax.psum(lon_terms, 'lon')  183 us
    all_gather x4, blocking collectives, surround(): lat_summed = jnp.sum(lax.all_gather(lat_terms, 'lat'), axis=0)  173 us
    ppermute x10, starting transfers between devices, padded_2(): lax.ppermute(head, axis, [((i + 1) % count, i) for i in range(ends)])  63.1 us
    all_gather x1, waiting for transfers between devices, surround(): lat_summed = jnp.sum(lax.all_gather(lat_terms, 'lat'), axis=0)  26.4 us
    ppermute x10, starting transfers between devices, padded_2(): lax.ppermute(tail, axis, [(i, (i + 1) % count) for i in range(ends)])  21 us
    gather x20, local copies, waits for them, and re-layouts, rim_terms(): picked = field[jnp.clip(target, 0, rows_dev - 1), cols_at + col_step]  19 us
    gather x20, local copies, waits for them, and re-layouts, rim_terms(): picked = field[rows_at + row_step, jnp.clip(target, 0, cols_dev - 1)]  15.7 us
    ppermute x5, waiting for transfers between devices, swapped(): return lax.ppermute(block, axis, route)  14.7 us
  transfers between devices with their start and end apart: 26, of which 6 were waited for; matrix products, arithmetic and copies ran while one was open for 2% of the time, Pallas kernels for 0%

profile of v1, /device:TPU:288, one launch (start us, length us, event | category | flops | bytes accessed | tf_op | source)
XLA Modules:
  0.0 581.9 jit_solution(17447674924875510925)
XLA Ops:
  10.4 1.6 gather_fusion.12
  23.2 43.9 %all_gather.21 = f32[16,2,1,32,128]{4,3,2,1,0:T(8,128)S(1)} all-gather(f32[1,2,1,32,128]{4,3,2,1,0:T(8,128)S(1)} %multiply_add_fusion.4), channel_id=1, replica_groups=mesh['panel'=2,'lon'=16,'lat'=16] {'lat'}, dimensions={0}, use_global_device_ids=true | all-gather | bytes 557056 | tf_op jit(solution)/shard_map/all_gather | solution.py:78
  67.3 45.8 %all-reduce.10 = (f32[2,2,16,128]{3,2,1,0:T(8,128)S(1)}, f32[2,1,16,128]{3,2,1,0:T(8,128)S(1)}) all-reduce(f32[2,2,16,128]{3,2,1,0:T(8,128)S(1)} %multiply_add_fusion.5, f32[2,1,16,128]{3,2,1,0:T(8,128)S(1)} %multiply_add_fusion.9), channel_id=1, replica_groups=mesh['panel'=2,'lon'=16,'lat'=16] {'lon'}, use_global_device_ids=true, to_apply=%region_2.3 | all-reduce | flops 12288 | bytes 98304 | tf_op jit(solution)/shard_map/psum | solution.py:79
  113.1 3.8 collective-permute-start.9
  116.9 1.9 collective-permute-start.5
  118.8 8.1 %collective-permute-start.6 = (f32[1,32,128]{2,1,0:T(8,128)S(1)}, f32[1,32,128]{2,1,0:T(8,128)S(1)}, u32[]{:S(2)}, u32[]{:S(2)}) collective-permute-start(f32[1,32,128]{2,1,0:T(8,128)S(1)} %get-tuple-element.292), channel_id=1, source_target_pairs={{1,0},{2,1},{3,2},{4,3},{5,4},{6,5},{7,6},{8,7},{9,8},{10,9},{11,1... | collective-permute-start | bytes 49160 | tf_op jit(solution)/shard_map/ppermute | solution.py:23
  127.1 1.2 gather_fusion.2
  133.1 1.9 collective-permute-start
  135.1 8.1 %collective-permute-start.1 = (f32[2,32,128]{2,1,0:T(8,128)S(1)}, f32[2,32,128]{2,1,0:T(8,128)S(1)}, u32[]{:S(2)}, u32[]{:S(2)}) collective-permute-start(f32[2,32,128]{2,1,0:T(8,128)S(1)} %get-tuple-element.290), channel_id=1, source_target_pairs={{1,0},{2,1},{3,2},{4,3},{5,4},{6,5},{7,6},{8,7},{9,8},{10,9},{11,1... | collective-permute-start | bytes 98312 | tf_op jit(solution)/shard_map/ppermute | solution.py:23
  144.7 1.9 collective-permute-start.7
  146.6 4.9 collective-permute-start.8
  152.9 1.9 collective-permute-start.2
  154.8 4.9 collective-permute-start.3
  159.7 1.4 scatter.74
  161.6 26.4 %all-gather.2.cloned.1.call-done = f32[16,2,2,32,128]{4,3,2,1,0:T(8,128)} async-done(((f32[1,2,2,32,128]{4,3,2,1,0:T(8,128)}), f32[16,2,2,32,128]{4,3,2,1,0:T(8,128)}) %all-gather.2.cloned.1.call-update) | async-done | bytes 1048592 | tf_op jit(solution)/shard_map/all_gather | solution.py:78
  188.0 1.3 reduce_sum.53
  189.4 2.5 collective-permute-start.4
  191.8 1.3 constant_dynamic-slice_fusion
  193.1 2.8 collective-permute-done.4
  196.7 1.5 scatter.66
  200.4 1.3 copy_divide_fusion.1
  209.5 45.7 %all_gather.22 = f32[16,2,1,32,128]{4,3,2,1,0:T(8,128)S(1)} all-gather(f32[1,2,1,32,128]{4,3,2,1,0:T(8,128)S(1)} %multiply_add_fusion.3), channel_id=1, replica_groups=mesh['panel'=2,'lon'=16,'lat'=16] {'lat'}, dimensions={0}, use_global_device_ids=true | all-gather | bytes 557056 | tf_op jit(solution)/shard_map/all_gather | solution.py:78
  255.2 1.9 collective-permute-start.10
  257.1 8.1 %collective-permute-start.11 = (f32[1,32,128]{2,0,1:T(1,128)}, f32[1,32,128]{2,0,1:T(1,128)S(1)}, u32[]{:S(2)}, u32[]{:S(2)}) collective-permute-start(f32[1,32,128]{2,0,1:T(1,128)} %slice.1290), channel_id=1, source_target_pairs={{1,0},{2,1},{3,2},{4,3},{5,4},{6,5},{7,6},{8,7},{9,8},{10,9},{11,1... | collective-permute-start | bytes 49160 | tf_op jit(solution)/shard_map/ppermute | solution.py:23
  266.7 45.7 %psum.37 = f32[2,1,16,128]{3,2,1,0:T(8,128)S(1)} all-reduce(f32[2,1,16,128]{3,2,1,0:T(8,128)S(1)} %multiply_add_fusion.8), channel_id=1, replica_groups=mesh['panel'=2,'lon'=16,'lat'=16] {'lon'}, use_global_device_ids=true, to_apply=%region_6.7 | all-reduce | flops 4096 | bytes 32768 | tf_op jit(solution)/shard_map/psum | solution.py:79
  312.5 1.9 collective-permute-start.12
  314.4 4.9 collective-permute-start.13
  319.3 1.9 collective-permute-start.14
  321.3 4.0 collective-permute-done.14
  325.3 1.3 scatter.80
  337.4 42.4 %all_gather.23 = f32[16,2,1,32,128]{4,3,2,1,0:T(8,128)S(1)} all-gather(f32[1,2,1,32,128]{4,3,2,1,0:T(8,128)S(1)} %multiply_add_fusion.2), channel_id=1, replica_groups=mesh['panel'=2,'lon'=16,'lat'=16] {'lat'}, dimensions={0}, use_global_device_ids=true | all-gather | bytes 557056 | tf_op jit(solution)/shard_map/all_gather | solution.py:78
  379.8 2.4 collective-permute-start.15
  382.2 7.7 %collective-permute-start.16 = (f32[1,32,128]{2,0,1:T(1,128)}, f32[1,32,128]{2,0,1:T(1,128)S(1)}, u32[]{:S(2)}, u32[]{:S(2)}) collective-permute-start(f32[1,32,128]{2,0,1:T(1,128)} %slice.1305), channel_id=1, source_target_pairs={{1,0},{2,1},{3,2},{4,3},{5,4},{6,5},{7,6},{8,7},{9,8},{10,9},{11,1... | collective-permute-start | bytes 49160 | tf_op jit(solution)/shard_map/ppermute | solution.py:23
  391.4 45.7 %psum.38 = f32[2,1,16,128]{3,2,1,0:T(8,128)S(1)} all-reduce(f32[2,1,16,128]{3,2,1,0:T(8,128)S(1)} %multiply_add_fusion.7), channel_id=1, replica_groups=mesh['panel'=2,'lon'=16,'lat'=16] {'lon'}, use_global_device_ids=true, to_apply=%region_8.9 | all-reduce | flops 4096 | bytes 32768 | tf_op jit(solution)/shard_map/psum | solution.py:79
  437.1 1.9 collective-permute-start.17
  439.1 4.9 collective-permute-start.18
  443.9 1.9 collective-permute-start.19
  445.9 4.0 collective-permute-done.19
  449.9 1.3 scatter.86
  460.8 41.4 %all_gather.24 = f32[16,2,1,32,128]{4,3,2,1,0:T(8,128)S(1)} all-gather(f32[1,2,1,32,128]{4,3,2,1,0:T(8,128)S(1)} %multiply_add_fusion.1), channel_id=1, replica_groups=mesh['panel'=2,'lon'=16,'lat'=16] {'lat'}, dimensions={0}, use_global_device_ids=true | all-gather | bytes 557056 | tf_op jit(solution)/shard_map/all_gather | solution.py:78
  502.2 3.3 collective-permute-start.20
  505.5 6.8 %collective-permute-start.21 = (f32[1,32,128]{2,1,0:T(8,128)S(1)}, f32[1,32,128]{2,1,0:T(8,128)S(1)}, u32[]{:S(2)}, u32[]{:S(2)}) collective-permute-start(f32[1,32,128]{2,1,0:T(8,128)S(1)} %get-tuple-element.288), channel_id=1, source_target_pairs={{1,0},{2,1},{3,2},{4,3},{5,4},{6,5},{7,6},{8,7},{9,8},{10,9},{11,1... | collective-permute-start | bytes 49160 | tf_op jit(solution)/shard_map/ppermute | solution.py:23
  513.1 45.7 %psum.39 = f32[2,1,16,128]{3,2,1,0:T(8,128)S(1)} all-reduce(f32[2,1,16,128]{3,2,1,0:T(8,128)S(1)} %multiply_add_fusion.6), channel_id=1, replica_groups=mesh['panel'=2,'lon'=16,'lat'=16] {'lon'}, use_global_device_ids=true, to_apply=%region_10.11 | all-reduce | flops 4096 | bytes 32768 | tf_op jit(solution)/shard_map/psum | solution.py:79
  558.9 1.9 collective-permute-start.22
  560.8 4.9 collective-permute-start.23
  565.7 1.9 collective-permute-start.24
  567.7 4.0 collective-permute-done.24
  571.6 1.4 scatter.94
  (281 shorter events, 59.4 us)
Async XLA Ops:
  7.2 4.8 copy-start.2
  7.2 180.8 %all-gather.2.cloned.1.call-start = ((), (), s32[]{:S(2)}) async-start(), calls=%async_computation | async-start | bytes 1114112 | tf_op jit(solution)/shard_map/all_gather | solution.py:78
  9.4 57.7 %copy-start.19 = (f32[2,1,16]{2,1,0:T(1,128)}, f32[2,1,16]{2,1,0:T(1,128)S(1)}, u32[]{:S(2)}) copy-start(f32[2,1,16]{2,1,0:T(1,128)S(1)} %get-tuple-element.258) | copy-start | bytes 388
  10.1 56.9 %copy-start.7 = (f32[2,1,16]{2,1,0:T(1,128)}, f32[2,1,16]{2,1,0:T(1,128)S(1)}, u32[]{:S(2)}) copy-start(f32[2,1,16]{2,1,0:T(1,128)S(1)} %get-tuple-element.304) | copy-start | bytes 388
  12.0 2.6 copy-start
  17.4 0.9 copy-start.24
  18.3 0.7 copy-start.25
  19.0 190.4 %copy-start.21 = (f32[2,1,32]{2,1,0:T(1,128)}, f32[2,1,32]{2,1,0:T(1,128)S(1)}, u32[]{:S(2)}) copy-start(f32[2,1,32]{2,1,0:T(1,128)S(1)} %get-tuple-element.248) | copy-start | bytes 772
  19.0 190.3 %copy-start.10 = (f32[2,1,32]{2,1,0:T(1,128)}, f32[2,1,32]{2,1,0:T(1,128)S(1)}, u32[]{:S(2)}) copy-start(f32[2,1,32]{2,1,0:T(1,128)S(1)} %get-tuple-element.299) | copy-start | bytes 772
  19.0 190.3 %copy-start.13 = (f32[2,1,32]{2,1,0:T(1,128)}, f32[2,1,32]{2,1,0:T(1,128)S(1)}, u32[]{:S(2)}) copy-start(f32[2,1,32]{2,1,0:T(1,128)S(1)} %get-tuple-element.300) | copy-start | bytes 772
  19.1 190.3 %copy-start.16 = (f32[2,1,32]{2,1,0:T(1,128)}, f32[2,1,32]{2,1,0:T(1,128)S(1)}, u32[]{:S(2)}) copy-start(f32[2,1,32]{2,1,0:T(1,128)S(1)} %get-tuple-element.301) | copy-start | bytes 772
  113.1 46.6 %collective-permute-start.9 = (f32[2,1,48,128]{3,2,1,0:T(8,128)S(1)}, f32[2,1,48,128]{3,2,1,0:T(8,128)S(1)}, u32[]{:S(2)}, u32[]{:S(2)}) collective-permute-start(f32[2,1,48,128]{3,2,1,0:T(8,128)S(1)} %pad_maximum_fusion.6), channel_id=1, source_target_pairs={{0,256},{256,0},{1,257},{257,1},{2,258},{258,2},{3,259},{259,3},{4... | collective-permute-start | bytes 147464 | tf_op jit(solution)/shard_map/ppermute | solution.py:37
  116.9 27.7 %collective-permute-start.5 = (f32[1,32,128]{2,1,0:T(8,128)S(1)}, f32[1,32,128]{2,1,0:T(8,128)S(1)}, u32[]{:S(2)}, u32[]{:S(2)}) collective-permute-start(f32[1,32,128]{2,1,0:T(8,128)S(1)} %get-tuple-element.291), channel_id=1, source_target_pairs={{0,1},{1,2},{2,3},{3,4},{4,5},{5,6},{6,7},{7,8},{8,9},{9,10},{10,1... | collective-permute-start | bytes 49160 | tf_op jit(solution)/shard_map/ppermute | solution.py:21
  118.8 25.8 %collective-permute-start.6 = (f32[1,32,128]{2,1,0:T(8,128)S(1)}, f32[1,32,128]{2,1,0:T(8,128)S(1)}, u32[]{:S(2)}, u32[]{:S(2)}) collective-permute-start(f32[1,32,128]{2,1,0:T(8,128)S(1)} %get-tuple-element.292), channel_id=1, source_target_pairs={{1,0},{2,1},{3,2},{4,3},{5,4},{6,5},{7,6},{8,7},{9,8},{10,9},{11,1... | collective-permute-start | bytes 49160 | tf_op jit(solution)/shard_map/ppermute | solution.py:23
  133.1 19.7 %collective-permute-start = (f32[2,32,128]{2,0,1:T(2,128)S(1)}, f32[2,32,128]{2,0,1:T(2,128)S(1)}, u32[]{:S(2)}, u32[]{:S(2)}) collective-permute-start(f32[2,32,128]{2,0,1:T(2,128)S(1)} %bitcast.440), channel_id=1, source_target_pairs={{0,1},{1,2},{2,3},{3,4},{4,5},{5,6},{6,7},{7,8},{8,9},{9,10},{10,1... | collective-permute-start | bytes 98312 | tf_op jit(solution)/shard_map/ppermute | solution.py:21
  135.1 8.2 %copy-start.27 = (s32[3]{0:T(128)S(1)}, s32[3]{0:T(128)}, u32[]{:S(2)}) copy-start(s32[3]{0:T(128)} %constant.643.clone.1) | copy-start | bytes 40
  135.1 17.8 %collective-permute-start.1 = (f32[2,32,128]{2,1,0:T(8,128)S(1)}, f32[2,32,128]{2,1,0:T(8,128)S(1)}, u32[]{:S(2)}, u32[]{:S(2)}) collective-permute-start(f32[2,32,128]{2,1,0:T(8,128)S(1)} %get-tuple-element.290), channel_id=1, source_target_pairs={{1,0},{2,1},{3,2},{4,3},{5,4},{6,5},{7,6},{8,7},{9,8},{10,9},{11,1... | collective-permute-start | bytes 98312 | tf_op jit(solution)/shard_map/ppermute | solution.py:23
  144.7 7.4 %collective-permute-start.7 = (f32[18,1,128]{2,1,0:T(1,128)S(1)}, f32[18,1,128]{2,1,0:T(1,128)S(1)}, u32[]{:S(2)}, u32[]{:S(2)}) collective-permute-start(f32[18,1,128]{2,1,0:T(1,128)S(1)} %get-tuple-element.283), channel_id=1, source_target_pairs={{0,16},{16,32},{32,48},{48,64},{64,80},{80,96},{96,112},{112,128},... | collective-permute-start | bytes 27656 | tf_op jit(solution)/shard_map/ppermute | solution.py:21
  146.6 6.2 %collective-permute-start.8 = (f32[18,1,128]{2,1,0:T(1,128)S(1)}, f32[18,1,128]{2,1,0:T(1,128)S(1)}, u32[]{:S(2)}, u32[]{:S(2)}) collective-permute-start(f32[18,1,128]{2,1,0:T(1,128)S(1)} %get-tuple-element.284), channel_id=1, source_target_pairs={{16,0},{32,16},{48,32},{64,48},{80,64},{96,80},{112,96},{128,112},... | collective-permute-start | bytes 27656 | tf_op jit(solution)/shard_map/ppermute | solution.py:23
  152.9 8.6 %collective-permute-start.2 = (f32[20,2,128]{2,1,0:T(2,128)S(1)}, f32[20,2,128]{2,1,0:T(2,128)S(1)}, u32[]{:S(2)}, u32[]{:S(2)}) collective-permute-start(f32[20,2,128]{2,1,0:T(2,128)S(1)} %get-tuple-element.275), channel_id=1, source_target_pairs={{0,16},{16,32},{32,48},{48,64},{64,80},{80,96},{96,112},{112,128},... | collective-permute-start | bytes 61448 | tf_op jit(solution)/shard_map/ppermute | solution.py:21
  154.8 6.7 %collective-permute-start.3 = (f32[20,2,128]{2,1,0:T(2,128)S(1)}, f32[20,2,128]{2,1,0:T(2,128)S(1)}, u32[]{:S(2)}, u32[]{:S(2)}) collective-permute-start(f32[20,2,128]{2,1,0:T(2,128)S(1)} %get-tuple-element.276), channel_id=1, source_target_pairs={{16,0},{32,16},{48,32},{64,48},{80,64},{96,80},{112,96},{128,112},... | collective-permute-start | bytes 61448 | tf_op jit(solution)/shard_map/ppermute | solution.py:23
  189.4 6.5 %collective-permute-start.4 = (f32[2,2,48,128]{3,1,2,0:T(2,128)S(1)}, f32[2,2,48,128]{3,1,2,0:T(2,128)S(1)}, u32[]{:S(2)}, u32[]{:S(2)}) collective-permute-start(f32[2,2,48,128]{3,1,2,0:T(2,128)S(1)} %pad_maximum_fusion.5), channel_id=1, source_target_pairs={{0,256},{256,0},{1,257},{257,1},{2,258},{258,2},{3,259},{259,3},{4... | collective-permute-start | bytes 294920 | tf_op jit(solution)/shard_map/ppermute | solution.py:37
  199.0 1.0 copy-start.3
  199.1 1.0 copy-start.6
  255.2 57.3 %collective-permute-start.10 = (f32[1,32,128]{2,1,0:T(8,128)}, f32[1,32,128]{2,1,0:T(8,128)S(1)}, u32[]{:S(2)}, u32[]{:S(2)}) collective-permute-start(f32[1,32,128]{2,1,0:T(8,128)} %slice.1289), channel_id=1, source_target_pairs={{0,1},{1,2},{2,3},{3,4},{4,5},{5,6},{6,7},{7,8},{8,9},{9,10},{10,1... | collective-permute-start | bytes 49160 | tf_op jit(solution)/shard_map/ppermute | solution.py:21
  257.1 55.3 %collective-permute-start.11 = (f32[1,32,128]{2,0,1:T(1,128)}, f32[1,32,128]{2,0,1:T(1,128)S(1)}, u32[]{:S(2)}, u32[]{:S(2)}) collective-permute-start(f32[1,32,128]{2,0,1:T(1,128)} %slice.1290), channel_id=1, source_target_pairs={{1,0},{2,1},{3,2},{4,3},{5,4},{6,5},{7,6},{8,7},{9,8},{10,9},{11,1... | collective-permute-start | bytes 49160 | tf_op jit(solution)/shard_map/ppermute | solution.py:23
  312.5 8.7 %collective-permute-start.12 = (f32[18,1,128]{2,0,1:T(8,128)S(1)}, f32[18,1,128]{2,0,1:T(8,128)S(1)}, u32[]{:S(2)}, u32[]{:S(2)}) collective-permute-start(f32[18,1,128]{2,0,1:T(8,128)S(1)} %get-tuple-element.281), channel_id=1, source_target_pairs={{0,16},{16,32},{32,48},{48,64},{64,80},{80,96},{96,112},{112,128},... | collective-permute-start | bytes 27656 | tf_op jit(solution)/shard_map/ppermute | solution.py:21
  314.4 6.8 %collective-permute-start.13 = (f32[18,1,128]{2,0,1:T(8,128)S(1)}, f32[18,1,128]{2,0,1:T(8,128)S(1)}, u32[]{:S(2)}, u32[]{:S(2)}) collective-permute-start(f32[18,1,128]{2,0,1:T(8,128)S(1)} %get-tuple-element.282), channel_id=1, source_target_pairs={{16,0},{32,16},{48,32},{64,48},{80,64},{96,80},{112,96},{128,112},... | collective-permute-start | bytes 27656 | tf_op jit(solution)/shard_map/ppermute | solution.py:23
  319.3 6.0 %collective-permute-start.14 = (f32[2,1,48,128]{3,2,1,0:T(8,128)S(1)}, f32[2,1,48,128]{3,2,1,0:T(8,128)S(1)}, u32[]{:S(2)}, u32[]{:S(2)}) collective-permute-start(f32[2,1,48,128]{3,2,1,0:T(8,128)S(1)} %pad_maximum_fusion.7), channel_id=1, source_target_pairs={{0,256},{256,0},{1,257},{257,1},{2,258},{258,2},{3,259},{259,3},{4... | collective-permute-start | bytes 147464 | tf_op jit(solution)/shard_map/ppermute | solution.py:37
  327.3 1.0 copy-start.4
  334.7 2.0 copy-start.14
  334.7 1.9 copy-start.17
  334.7 1.9 copy-start.22
  379.8 57.3 %collective-permute-start.15 = (f32[1,32,128]{2,1,0:T(8,128)}, f32[1,32,128]{2,1,0:T(8,128)S(1)}, u32[]{:S(2)}, u32[]{:S(2)}) collective-permute-start(f32[1,32,128]{2,1,0:T(8,128)} %slice.1304), channel_id=1, source_target_pairs={{0,1},{1,2},{2,3},{3,4},{4,5},{5,6},{6,7},{7,8},{8,9},{9,10},{10,1... | collective-permute-start | bytes 49160 | tf_op jit(solution)/shard_map/ppermute | solution.py:21
  382.2 54.9 %collective-permute-start.16 = (f32[1,32,128]{2,0,1:T(1,128)}, f32[1,32,128]{2,0,1:T(1,128)S(1)}, u32[]{:S(2)}, u32[]{:S(2)}) collective-permute-start(f32[1,32,128]{2,0,1:T(1,128)} %slice.1305), channel_id=1, source_target_pairs={{1,0},{2,1},{3,2},{4,3},{5,4},{6,5},{7,6},{8,7},{9,8},{10,9},{11,1... | collective-permute-start | bytes 49160 | tf_op jit(solution)/shard_map/ppermute | solution.py:23
  437.1 8.7 %collective-permute-start.17 = (f32[18,1,128]{2,0,1:T(8,128)S(1)}, f32[18,1,128]{2,0,1:T(8,128)S(1)}, u32[]{:S(2)}, u32[]{:S(2)}) collective-permute-start(f32[18,1,128]{2,0,1:T(8,128)S(1)} %get-tuple-element.279), channel_id=1, source_target_pairs={{0,16},{16,32},{32,48},{48,64},{64,80},{80,96},{96,112},{112,128},... | collective-permute-start | bytes 27656 | tf_op jit(solution)/shard_map/ppermute | solution.py:21
  439.1 6.8 %collective-permute-start.18 = (f32[18,1,128]{2,0,1:T(8,128)S(1)}, f32[18,1,128]{2,0,1:T(8,128)S(1)}, u32[]{:S(2)}, u32[]{:S(2)}) collective-permute-start(f32[18,1,128]{2,0,1:T(8,128)S(1)} %get-tuple-element.280), channel_id=1, source_target_pairs={{16,0},{32,16},{48,32},{64,48},{80,64},{96,80},{112,96},{128,112},... | collective-permute-start | bytes 27656 | tf_op jit(solution)/shard_map/ppermute | solution.py:23
  443.9 6.0 %collective-permute-start.19 = (f32[2,1,48,128]{3,2,1,0:T(8,128)S(1)}, f32[2,1,48,128]{3,2,1,0:T(8,128)S(1)}, u32[]{:S(2)}, u32[]{:S(2)}) collective-permute-start(f32[2,1,48,128]{3,2,1,0:T(8,128)S(1)} %pad_maximum_fusion.8), channel_id=1, source_target_pairs={{0,256},{256,0},{1,257},{257,1},{2,258},{258,2},{3,259},{259,3},{4... | collective-permute-start | bytes 147464 | tf_op jit(solution)/shard_map/ppermute | solution.py:37
  452.5 1.0 copy-start.5
  453.6 114.0 %copy-start.1 = (f32[16,32,128]{2,1,0:T(8,128)}, f32[16,32,128]{2,1,0:T(8,128)S(1)}, u32[]{:S(2)}) copy-start(f32[16,32,128]{2,1,0:T(8,128)S(1)} %copy_divide_fusion) | copy-start | bytes 786436
  459.3 0.8 copy-start.15
  459.3 0.8 copy-start.18
  459.3 0.8 copy-start.23
  502.2 56.6 %collective-permute-start.20 = (f32[1,32,128]{2,1,0:T(8,128)S(1)}, f32[1,32,128]{2,1,0:T(8,128)S(1)}, u32[]{:S(2)}, u32[]{:S(2)}) collective-permute-start(f32[1,32,128]{2,1,0:T(8,128)S(1)} %get-tuple-element.287), channel_id=1, source_target_pairs={{0,1},{1,2},{2,3},{3,4},{4,5},{5,6},{6,7},{7,8},{8,9},{9,10},{10,1... | collective-permute-start | bytes 49160 | tf_op jit(solution)/shard_map/ppermute | solution.py:21
  505.5 53.3 %collective-permute-start.21 = (f32[1,32,128]{2,1,0:T(8,128)S(1)}, f32[1,32,128]{2,1,0:T(8,128)S(1)}, u32[]{:S(2)}, u32[]{:S(2)}) collective-permute-start(f32[1,32,128]{2,1,0:T(8,128)S(1)} %get-tuple-element.288), channel_id=1, source_target_pairs={{1,0},{2,1},{3,2},{4,3},{5,4},{6,5},{7,6},{8,7},{9,8},{10,9},{11,1... | collective-permute-start | bytes 49160 | tf_op jit(solution)/shard_map/ppermute | solution.py:23
  558.9 8.7 %collective-permute-start.22 = (f32[18,1,128]{2,1,0:T(1,128)S(1)}, f32[18,1,128]{2,1,0:T(1,128)S(1)}, u32[]{:S(2)}, u32[]{:S(2)}) collective-permute-start(f32[18,1,128]{2,1,0:T(1,128)S(1)} %get-tuple-element.277), channel_id=1, source_target_pairs={{0,16},{16,32},{32,48},{48,64},{64,80},{80,96},{96,112},{112,128},... | collective-permute-start | bytes 27656 | tf_op jit(solution)/shard_map/ppermute | solution.py:21
  560.8 6.8 %collective-permute-start.23 = (f32[18,1,128]{2,1,0:T(1,128)S(1)}, f32[18,1,128]{2,1,0:T(1,128)S(1)}, u32[]{:S(2)}, u32[]{:S(2)}) collective-permute-start(f32[18,1,128]{2,1,0:T(1,128)S(1)} %get-tuple-element.278), channel_id=1, source_target_pairs={{16,0},{32,16},{48,32},{64,48},{80,64},{96,80},{112,96},{128,112},... | collective-permute-start | bytes 27656 | tf_op jit(solution)/shard_map/ppermute | solution.py:23
  565.7 6.0 %collective-permute-start.24 = (f32[2,1,48,128]{3,2,1,0:T(8,128)S(1)}, f32[2,1,48,128]{3,2,1,0:T(8,128)S(1)}, u32[]{:S(2)}, u32[]{:S(2)}) collective-permute-start(f32[2,1,48,128]{3,2,1,0:T(8,128)S(1)} %pad_maximum_fusion.9), channel_id=1, source_target_pairs={{0,256},{256,0},{1,257},{257,1},{2,258},{258,2},{3,259},{259,3},{4... | collective-permute-start | bytes 147464 | tf_op jit(solution)/shard_map/ppermute | solution.py:37
  (6 other events, 4.0 us)
Sparse Core Ops, SparseCore 0:
  133.2 54.7 all-gather.1
